TPU v7x, 512 devices: a whole 4x4x16 slice. The times are simulated.
512 devices in a mesh: row: 32 (over x, y, core), col: 16 (over z).
Axes of the slice: x: 4, y: 4, z: 16, core: 2. Of those that a mesh axis runs over, the one named last changes fastest.
Arguments:
- features: bfloat16 [65536, 256], P('col', 'row'), may hold values from -6 to 6
- weight: bfloat16 [256, 256], replicated, may hold values from -0.375 to 0.375
- adj_values: bfloat16 [32, 16, 96, 128, 128], P('row', 'col'), may hold values from -0.0625 to 0.0625
- block_rows: int32 [32, 16, 96], P('row', 'col'), may hold values from 0 to 15, as said below
- block_cols: int32 [32, 16, 96], P('row', 'col'), may hold values from 0 to 31
- block_counts: int32 [32, 16], P('row', 'col'), may hold values from 1 to 96, as said below
- cotangent: bfloat16 [65536, 256], P(('row', 'col')), may hold values from -6 to 6
Outputs:
- output: bfloat16 [65536, 256], P(('row', 'col'))
- grad_weight: float32 [256, 256], replicated
- grad_features: bfloat16 [65536, 256], P('col', 'row')
Inputs may be any that keep to these rules, and one draw needn't show every extreme that they name: Within one tile the pairs (block_rows, block_cols) over all 96 slots are distinct. `block_counts`: some tile holds exactly 96 live blocks and some other tile exactly one in every draw.
All inputs are finite; a program needn't handle non-finite values.
Results may differ from a plain program's by a relative error of at most 0.029.
Values may be sent and summed in bfloat16 or wider, within the bound.
A program may use at most 64 MiB of HBM per device.

v0:
```python
import math
import jax
import jax.numpy as jnp
from jax import lax
from jax.sharding import PartitionSpec as P

RB = 16


def block_product(tile_values, tile_rows, tile_cols, live_count, panels, out_blocks, transposed):
    padded = tile_values.shape[0]
    blocks_turn = math.gcd(padded, 16)
    block_size = panels.shape[1]
    columns = panels.shape[2]
    turns_needed = (live_count + blocks_turn - 1) // blocks_turn

    def step(turn_index, running):
        offset = turn_index * blocks_turn
        values_now = lax.dynamic_slice_in_dim(tile_values, offset, blocks_turn, 0)
        row_ids = lax.dynamic_slice_in_dim(tile_rows, offset, blocks_turn, 0)
        col_ids = lax.dynamic_slice_in_dim(tile_cols, offset, blocks_turn, 0)
        is_live = offset + jnp.arange(blocks_turn, dtype=jnp.int32) < live_count
        if transposed:
            picked = jnp.take(panels, row_ids, axis=0)
            product = jnp.einsum(
                "bij,bif->bjf", values_now, picked, preferred_element_type=jnp.float32
            )
            target_ids = col_ids
        else:
            picked = jnp.take(panels, col_ids, axis=0)
            product = jnp.einsum(
                "bij,bjf->bif", values_now, picked, preferred_element_type=jnp.float32
            )
            target_ids = row_ids
        contribution = jnp.where(is_live[:, None, None], product, 0.0)
        return running.at[target_ids].add(contribution)

    start_sum = jnp.zeros((out_blocks, block_size, columns), jnp.float32)
    return lax.fori_loop(0, turns_needed, step, start_sum)


def shards(features, weight, adj_values, block_rows, block_cols, block_counts, cotangent):
    tile_values = adj_values[0, 0]
    tile_rows = block_rows[0, 0]
    tile_cols = block_cols[0, 0]
    live_count = block_counts[0, 0]
    block_size = tile_values.shape[1]
    col_blocks = features.shape[0] // block_size
    node_total = col_blocks * block_size * lax.axis_size("col")
    panel_part = lax.all_gather(features, "row", axis=1, tiled=True)
    panels = panel_part.reshape(col_blocks, block_size, panel_part.shape[1])
    partial_value = block_product(tile_values, tile_rows, tile_cols, live_count, panels, RB, False)
    partial_value = partial_value.reshape(RB * block_size, partial_value.shape[2])
    aggregated = lax.psum_scatter(
        partial_value.astype(jnp.bfloat16), "col", scatter_dimension=0, tiled=True
    )
    preact = jnp.dot(aggregated, weight, preferred_element_type=jnp.float32)
    output = jax.nn.silu(preact).astype(jnp.bfloat16)
    sigmoid_pre = jax.nn.sigmoid(preact)
    slopes = sigmoid_pre * (1.0 + preact * (1.0 - sigmoid_pre))
    deltas = (cotangent.astype(jnp.float32) * slopes).astype(jnp.bfloat16)
    local_grad = jnp.dot(aggregated.T, deltas, preferred_element_type=jnp.float32)
    grad_weight = lax.psum(local_grad, ("row", "col")) * (1.0 / math.sqrt(node_total))
    backward = jnp.dot(deltas, weight.T, preferred_element_type=jnp.float32).astype(jnp.bfloat16)
    back_slab = lax.all_gather(backward, "col", axis=0, tiled=True)
    back_panels = back_slab.reshape(RB, block_size, back_slab.shape[1])
    column_terms = block_product(
        tile_values, tile_rows, tile_cols, live_count, back_panels, col_blocks, True
    )
    column_terms = column_terms.reshape(col_blocks * block_size, column_terms.shape[2])
    grad_features = lax.psum_scatter(
        column_terms.astype(jnp.bfloat16), "row", scatter_dimension=1, tiled=True
    )
    return (output, grad_weight, grad_features)


def solution(mesh):
    return jax.shard_map(
        shards,
        mesh=mesh,
        in_specs=(
            P("col", "row"),
            P(),
            P("row", "col", None, None, None),
            P("row", "col", None),
            P("row", "col", None),
            P("row", "col"),
            P(("row", "col"), None),
        ),
        out_specs=(P(("row", "col"), None), P(), P("col", "row")),
        check_vma=False,
    )
```

profile of v0, /device:TPU:2, one launch (start us, length us, event | category | flops | bytes accessed | tf_op | source)
XLA Modules:
  0.0 847.8 jit_solution(3140927563884392423)
XLA Ops:
  7.2 0.0 all-gather.3.cloned.1.call-start
  7.2 0.7 all-gather.3.cloned.1.call-update
  7.9 0.0 reduce-scatter.3.cloned.1.call-start
  8.6 65.7 %all-gather.3.cloned.1.call-done = bf16[4096,256]{0,1:T(8,128)(2,1)} async-done(((bf16[4096,8]{0,1:T(8,128)(2,1)}), bf16[4096,256]{0,1:T(8,128)(2,1)}) %all-gather.3.cloned.1.call-update) | async-done | bytes 2097168 | tf_op jit(solution)/shard_map/all_gather | solution.py:50
  74.3 4.1 copy.11
  78.4 1.5 broadcast_in_dim.58
  80.0 35.9 %while.20 = (s32[]{:T(128)}, f32[16,128,256]{2,1,0:T(8,128)}, s32[]{:T(128)}, s32[96]{0:T(128)S(1)}, s32[]{:T(128)}, /*index=5*/bf16[96,128,128]{2,1,0:T(8,128)(...) while((s32[]{:T(128)}, f32[16,128,256]{2,1,0:T(8,128)}, ...), condition=%wide.region_2.3_spmd, body=%wide.region_0.2_spmd.sunk | while | flops 135791792 | bytes 12063415 | solution.py:39
  80.0 0.7 compare_and_fusion.4
  80.7 2.2 gather_fusion
  82.9 1.5 convolution_select_fusion.4
  84.5 0.1 compare_select_fusion.8
  84.5 4.3 scatter_fusion
  88.9 0.7 compare_and_fusion.4
  89.6 2.2 gather_fusion
  91.8 1.6 convolution_select_fusion.4
  93.4 0.1 compare_select_fusion.8
  93.4 4.4 scatter_fusion
  97.8 0.7 compare_and_fusion.4
  98.5 2.2 gather_fusion
  100.8 1.5 convolution_select_fusion.4
  102.3 0.1 compare_select_fusion.8
  102.4 4.5 scatter_fusion
  106.8 0.7 compare_and_fusion.4
  107.6 2.2 gather_fusion
  109.8 1.6 convolution_select_fusion.4
  111.4 0.1 compare_select_fusion.8
  111.4 4.4 scatter_fusion
  115.9 2.8 convert_element_type.24
  118.7 0.0 all-gather.5.cloned.1.call-start
  118.8 87.5 %reduce-scatter.3.cloned.1.call-done = bf16[128,256]{1,0:T(8,128)(2,1)} async-done(((bf16[2048,256]{1,0:T(8,128)(2,1)}), bf16[128,256]{1,0:T(8,128)(2,1)}) %reduce-scatter.3.cloned.1.call-update) | async-done | bytes 65552 | tf_op jit(solution)/shard_map/reduce_scatter | solution.py:54
  206.3 1.7 multiply_convert_fusion
  208.0 0.8 convolution_convert_fusion
  208.9 0.0 all-reduce.2.cloned.1.call-start
  208.9 2.8 copy.10
  211.7 0.9 fusion.12
  212.7 0.0 reduce-scatter.5.cloned.1.call-start
  212.7 65.3 %all-gather.5.cloned.1.call-done = bf16[2048,256]{1,0:T(8,128)(2,1)} async-done(((bf16[128,256]{1,0:T(8,128)(2,1)}), bf16[2048,256]{1,0:T(8,128)(2,1)}) %all-gather.5.cloned.1.call-update) | async-done | bytes 1048592 | tf_op jit(solution)/shard_map/all_gather | solution.py:65
  278.1 2.4 broadcast_in_dim.59
  280.5 34.6 %while.21 = (s32[]{:T(128)}, f32[32,128,256]{2,1,0:T(8,128)}, s32[]{:T(128)}, s32[96]{0:T(128)S(1)}, s32[]{:T(128)}, /*index=5*/bf16[96,128,128]{1,2,0:T(8,128)(...) while((s32[]{:T(128)}, f32[32,128,256]{2,1,0:T(8,128)}, ...), condition=%wide.region_7.8_spmd, body=%wide.region_5.7_spmd.sunk | while | flops 135791792 | bytes 12063415 | solution.py:39
  280.5 0.7 compare_and_fusion.5
  281.2 1.8 gather_fusion.1
  283.1 1.6 convolution_select_fusion.5
  284.6 0.1 compare_select_fusion.9
  284.7 4.3 scatter_fusion.1
  289.1 0.7 compare_and_fusion.5
  289.8 1.8 gather_fusion.1
  291.6 1.5 convolution_select_fusion.5
  293.2 0.1 compare_select_fusion.9
  293.3 4.5 scatter_fusion.1
  297.7 0.7 compare_and_fusion.5
  298.5 1.8 gather_fusion.1
  300.3 1.6 convolution_select_fusion.5
  301.9 0.1 compare_select_fusion.9
  301.9 4.5 scatter_fusion.1
  306.4 0.7 compare_and_fusion.5
  307.1 1.8 gather_fusion.1
  309.0 1.6 convolution_select_fusion.5
  310.5 0.1 compare_select_fusion.9
  310.6 4.4 scatter_fusion.1
  315.1 2.5 convert_element_type.30
  317.6 2.9 copy.15
  320.5 418.5 %all-reduce.2.cloned.1.call-done = f32[256,256]{1,0:T(8,128)} async-done(((f32[256,256]{1,0:T(8,128)}), f32[256,256]{1,0:T(8,128)}) %all-reduce.2.cloned.1.call-update) | async-done | bytes 262160 | tf_op jit(solution)/shard_map/psum | solution.py:63
  739.0 1.7 broadcast_multiply_fusion
  740.6 100.6 %reduce-scatter.5.cloned.1.call-done = bf16[4096,8]{0,1:T(8,128)(2,1)} async-done(((bf16[4096,256]{0,1:T(8,128)(2,1)}), bf16[4096,8]{0,1:T(8,128)(2,1)}) %reduce-scatter.5.cloned.1.call-update) | async-done | bytes 65552 | tf_op jit(solution)/shard_map/reduce_scatter | solution.py:71
  (24 shorter events, 0.1 us)
Async XLA Ops:
  7.2 199.1 %copy-start = (bf16[256,256]{1,0:T(8,128)(2,1)S(1)}, bf16[256,256]{1,0:T(8,128)(2,1)}, u32[]{:S(2)}) copy-start(bf16[256,256]{1,0:T(8,128)(2,1)} %param.12) | copy-start | bytes 393220
  7.2 67.2 %all-gather.3.cloned.1.call-start = ((), (), s32[]{:S(2)}) async-start(), calls=%async_computation.2 | async-start | bytes 2162688 | tf_op jit(solution)/shard_map/all_gather | solution.py:50
  7.9 198.4 %reduce-scatter.3.cloned.1.call-start = ((), (), s32[]{:S(2)}) async-start(), calls=%async_computation.3 | async-start | bytes 1114112 | tf_op jit(solution)/shard_map/reduce_scatter | solution.py:54
  78.4 1.5 copy-start.3
  78.4 1.5 copy-start.4
  115.9 90.4 %copy-start.5 = (bf16[128,256]{1,0:T(8,128)(2,1)S(1)}, bf16[128,256]{1,0:T(8,128)(2,1)}, u32[]{:S(2)}) copy-start(bf16[128,256]{1,0:T(8,128)(2,1)} %param.17) | copy-start | bytes 196612
  115.9 93.1 %copy-start.1 = (bf16[96,128,128]{2,1,0:T(8,128)(2,1)S(1)}, bf16[96,128,128]{2,1,0:T(8,128)(2,1)}, u32[]{:S(2)}) copy-start(bf16[96,128,128]{2,1,0:T(8,128)(2,1)} %get-tuple-element.328) | copy-start | bytes 9437188
  118.7 159.3 %all-gather.5.cloned.1.call-start = ((), (), s32[]{:S(2)}) async-start(), calls=%async_computation.5 | async-start | bytes 1114112 | tf_op jit(solution)/shard_map/all_gather | solution.py:65
  208.9 2.9 copy-start.2
  208.9 530.1 %all-reduce.2.cloned.1.call-start = ((), (), s32[]{:S(2)}) async-start(), calls=%async_computation.4 | async-start | bytes 524288 | tf_op jit(solution)/shard_map/psum | solution.py:63
  212.7 628.6 %reduce-scatter.5.cloned.1.call-start = ((), (), s32[]{:S(2)}) async-start(), calls=%async_computation.6 | async-start | bytes 2162688 | tf_op jit(solution)/shard_map/reduce_scatter | solution.py:71
Sparse Core Ops, SparseCore 0:
  11.1 63.1 all-gather.2
  118.9 87.4 reduce-scatter.2
  209.2 68.8 all-gather.4
  284.8 454.1 all-reduce.1
  743.8 97.3 reduce-scatter.4
where the time goes:
time: 850 us; the launch traced here: 848 us
  waiting for transfers between devices  738 us (87%)
  other arithmetic  48.7 us (6%)
  local copies, waits for them, and re-layouts  30 us (4%)
  matrix products  15.8 us (2%)
  between operations  14.5 us (2%)
    psum x1, waiting for transfers between devices, shards(): lax.psum(local_grad, ('row', 'col')) * (1.0 / math.sqrt(node_total))  418 us
    reduce_scatter x1, waiting for transfers between devices, shards(): lax.psum_scatter(column_terms.astype(jnp.bfloat16), 'row', scatter_dimens...  101 us
    reduce_scatter x1, waiting for transfers between devices, shards(): lax.psum_scatter(partial_value.astype(jnp.bfloat16), 'col', scatter_dimen...  87.5 us
    all_gather x1, waiting for transfers between devices, shards(): panel_part = lax.all_gather(features, 'row', axis=1, tiled=True)  65.7 us
    all_gather x1, waiting for transfers between devices, shards(): back_slab = lax.all_gather(backward, 'col', axis=0, tiled=True)  65.3 us
    scatter-add x8, other arithmetic, step(): return running.at[target_ids].add(contribution)  35.2 us
  transfers between devices with their start and end apart: 5, of which 5 were waited for; matrix products, arithmetic and copies ran while one was open for 6% of the time, Pallas kernels for 0%

commit v1 on v0

--- a/solution.py
+++ b/solution.py
@@ -62,7 +62,11 @@
     local_grad = jnp.dot(aggregated.T, deltas, preferred_element_type=jnp.float32)
     grad_weight = lax.psum(local_grad, ("row", "col")) * (1.0 / math.sqrt(node_total))
     backward = jnp.dot(deltas, weight.T, preferred_element_type=jnp.float32).astype(jnp.bfloat16)
-    back_slab = lax.all_gather(backward, "col", axis=0, tiled=True)
+    full_n = jax.lax.axis_size("col")
+    pieces_in = [full_n if h == 0 else 1 for h in range(backward.ndim)]
+    back_slab = jax.lax.all_to_all(
+        jnp.tile(backward, pieces_in), "col", split_axis=0, tiled=True, concat_axis=0
+    )
     back_panels = back_slab.reshape(RB, block_size, back_slab.shape[1])
     column_terms = block_product(
         tile_values, tile_rows, tile_cols, live_count, back_panels, col_blocks, True

time: 850 us -> 799 us (0.940)
  waiting for transfers between devices: 738 us -> 679 us
  starting transfers between devices: 0.2 us -> 8.86 us
    all_gather x1 -> x0, waiting for transfers between devices: 65.3 us -> none  [shards(): back_slab = lax.all_gather(backward, 'col', axis=0, tiled=True)]
    all_to_all x0 -> x1, waiting for transfers between devices: none -> 36.9 us  [shards(): jax.lax.all_to_all(jnp.tile(backward, pieces_in), 'col', split_axis=0, ti...]
    psum x1, waiting for transfers between devices: 418 us -> 387 us  [shards(): lax.psum(local_grad, ('row', 'col')) * (1.0 / math.sqrt(node_total))]
    all_to_all x0 -> x1, starting transfers between devices: none -> 8.7 us  [shards(): jax.lax.all_to_all(jnp.tile(backward, pieces_in), 'col', split_axis=0, ti...]
where the time goes in v1:
time: 799 us; the launch traced here: 797 us
  waiting for transfers between devices  679 us (85%)
  other arithmetic  48.8 us (6%)
  local copies, waits for them, and re-layouts  31.1 us (4%)
  matrix products  15.2 us (2%)
  between operations  14.5 us (2%)
  starting transfers between devices  8.86 us (1%)
    psum x1, waiting for transfers between devices, shards(): lax.psum(local_grad, ('row', 'col')) * (1.0 / math.sqrt(node_total))  387 us
    reduce_scatter x1, waiting for transfers between devices, shards(): lax.psum_scatter(column_terms.astype(jnp.bfloat16), 'row', scatter_dimens...  101 us
    reduce_scatter x1, waiting for transfers between devices, shards(): lax.psum_scatter(partial_value.astype(jnp.bfloat16), 'col', scatter_dimen...  87.7 us
    all_gather x1, waiting for transfers between devices, shards(): panel_part = lax.all_gather(features, 'row', axis=1, tiled=True)  65.7 us
    all_to_all x1, waiting for transfers between devices, shards(): jax.lax.all_to_all(jnp.tile(backward, pieces_in), 'col', split_axis=0, ti...  36.9 us
    scatter-add x8, other arithmetic, step(): return running.at[target_ids].add(contribution)  35.4 us
  transfers between devices with their start and end apart: 5, of which 5 were waited for; matrix products, arithmetic and copies ran while one was open for 6% of the time, Pallas kernels for 0%

profile of v1, /device:TPU:2, one launch (start us, length us, event | category | flops | bytes accessed | tf_op | source)
XLA Modules:
  0.0 797.2 jit_solution(10319304800401131378)
XLA Ops:
  7.2 0.7 all-gather.2.cloned.1.call-update
  7.9 0.0 reduce-scatter.3.cloned.1.call-start
  8.6 65.7 %all-gather.2.cloned.1.call-done = bf16[4096,256]{0,1:T(8,128)(2,1)} async-done(((bf16[4096,8]{0,1:T(8,128)(2,1)}), bf16[4096,256]{0,1:T(8,128)(2,1)}) %all-gather.2.cloned.1.call-update) | async-done | bytes 2097168 | tf_op jit(solution)/shard_map/all_gather | solution.py:50
  74.3 4.1 copy.11
  78.4 1.5 broadcast_in_dim.58
  80.0 36.0 %while.20 = (s32[]{:T(128)}, f32[16,128,256]{2,1,0:T(8,128)}, s32[]{:T(128)}, s32[96]{0:T(128)S(1)}, s32[]{:T(128)}, /*index=5*/bf16[96,128,128]{2,1,0:T(8,128)(...) while((s32[]{:T(128)}, f32[16,128,256]{2,1,0:T(8,128)}, ...), condition=%wide.region_2.3_spmd, body=%wide.region_0.2_spmd.sunk | while | flops 135791792 | bytes 12063415 | solution.py:39
  80.0 0.7 compare_and_fusion.4
  80.7 2.2 gather_fusion
  82.9 1.6 convolution_select_fusion.4
  84.5 0.1 compare_select_fusion.8
  84.6 4.3 scatter_fusion
  88.9 0.7 compare_and_fusion.4
  89.6 2.2 gather_fusion
  91.8 1.6 convolution_select_fusion.4
  93.4 0.1 compare_select_fusion.8
  93.5 4.4 scatter_fusion
  97.9 0.7 compare_and_fusion.4
  98.6 2.2 gather_fusion
  100.8 1.5 convolution_select_fusion.4
  102.4 0.1 compare_select_fusion.8
  102.4 4.5 scatter_fusion
  106.9 0.7 compare_and_fusion.4
  107.6 2.2 gather_fusion
  109.8 1.6 convolution_select_fusion.4
  111.4 0.1 compare_select_fusion.8
  111.5 4.5 scatter_fusion
  115.9 2.7 convert_element_type.24
  118.7 87.7 %reduce-scatter.3.cloned.1.call-done = bf16[128,256]{1,0:T(8,128)(2,1)} async-done(((bf16[2048,256]{1,0:T(8,128)(2,1)}), bf16[128,256]{1,0:T(8,128)(2,1)}) %reduce-scatter.3.cloned.1.call-update) | async-done | bytes 65552 | tf_op jit(solution)/shard_map/reduce_scatter | solution.py:54
  206.4 1.7 multiply_convert_fusion
  208.1 0.2 convolution_convert_fusion
  208.3 1.1 tile.2
  209.4 8.7 %all-to-all-start = ((bf16[16,128,256]{2,1,0:T(8,128)(2,1)}), bf16[16,128,256]{2,1,0:T(8,128)(2,1)}, u32[]{:S(2)}, u32[]{:S(2)}) async-start(bf16[16,128,256]{2,1,0:T(8,128)(2,1)} %tile.2), calls=%async_computation.1 | async-start | bytes 2097152 | tf_op jit(solution)/shard_map/all_to_all | solution.py:67
  218.1 0.0 all-reduce.2.cloned.1.call-start
  218.2 2.8 copy.10
  221.0 0.9 fusion.12
  221.9 0.0 reduce-scatter.5.cloned.1.call-start
  222.0 36.9 %all-to-all-done = bf16[16,128,256]{2,1,0:T(8,128)(2,1)} async-done(((bf16[16,128,256]{2,1,0:T(8,128)(2,1)}), bf16[16,128,256]{2,1,0:T(8,128)(2,1)}, u32[]{:S(2)}, u32[]{:S(2)}) %all-to-all-start) | async-done | bytes 1048608 | tf_op jit(solution)/shard_map/all_to_all | solution.py:67
  258.8 2.4 broadcast_in_dim.59
  261.3 34.7 %while.21 = (s32[]{:T(128)}, f32[32,128,256]{2,1,0:T(8,128)}, s32[]{:T(128)}, s32[96]{0:T(128)S(1)}, s32[]{:T(128)}, /*index=5*/bf16[96,128,128]{1,2,0:T(8,128)(...) while((s32[]{:T(128)}, f32[32,128,256]{2,1,0:T(8,128)}, ...), condition=%wide.region_7.8_spmd, body=%wide.region_5.7_spmd.sunk | while | flops 135791792 | bytes 12063415 | solution.py:39
  261.3 0.7 compare_and_fusion.5
  262.0 1.8 gather_fusion.1
  263.9 1.6 convolution_select_fusion.5
  265.4 0.1 compare_select_fusion.9
  265.5 4.3 scatter_fusion.1
  269.9 0.7 compare_and_fusion.5
  270.6 1.8 gather_fusion.1
  272.4 1.5 convolution_select_fusion.5
  274.0 0.1 compare_select_fusion.9
  274.1 4.5 scatter_fusion.1
  278.5 0.7 compare_and_fusion.5
  279.3 1.8 gather_fusion.1
  281.1 1.6 convolution_select_fusion.5
  282.7 0.1 compare_select_fusion.9
  282.8 4.5 scatter_fusion.1
  287.3 0.7 compare_and_fusion.5
  288.0 1.8 gather_fusion.1
  289.9 1.6 convolution_select_fusion.5
  291.4 0.1 compare_select_fusion.9
  291.5 4.5 scatter_fusion.1
  296.0 2.5 convert_element_type.30
  298.5 3.0 copy.15
  301.4 387.0 %all-reduce.2.cloned.1.call-done = f32[256,256]{1,0:T(8,128)} async-done(((f32[256,256]{1,0:T(8,128)}), f32[256,256]{1,0:T(8,128)}) %all-reduce.2.cloned.1.call-update) | async-done | bytes 262160 | tf_op jit(solution)/shard_map/psum | solution.py:63
  688.4 1.7 broadcast_multiply_fusion
  690.1 100.6 %reduce-scatter.5.cloned.1.call-done = bf16[4096,8]{0,1:T(8,128)(2,1)} async-done(((bf16[4096,256]{0,1:T(8,128)(2,1)}), bf16[4096,8]{0,1:T(8,128)(2,1)}) %reduce-scatter.5.cloned.1.call-update) | async-done | bytes 65552 | tf_op jit(solution)/shard_map/reduce_scatter | solution.py:75
  (24 shorter events, 0.2 us)
Async XLA Ops:
  7.2 199.2 %copy-start = (bf16[256,256]{1,0:T(8,128)(2,1)S(1)}, bf16[256,256]{1,0:T(8,128)(2,1)}, u32[]{:S(2)}) copy-start(bf16[256,256]{1,0:T(8,128)(2,1)} %param.12) | copy-start | bytes 393220
  7.2 67.2 %all-gather.2.cloned.1.call-start = ((), (), s32[]{:S(2)}) async-start(), calls=%async_computation.3 | async-start | bytes 2162688 | tf_op jit(solution)/shard_map/all_gather | solution.py:50
  7.9 198.5 %reduce-scatter.3.cloned.1.call-start = ((), (), s32[]{:S(2)}) async-start(), calls=%async_computation.4 | async-start | bytes 1114112 | tf_op jit(solution)/shard_map/reduce_scatter | solution.py:54
  78.4 1.5 copy-start.3
  78.4 1.5 copy-start.4
  115.9 90.5 %copy-start.5 = (bf16[128,256]{1,0:T(8,128)(2,1)S(1)}, bf16[128,256]{1,0:T(8,128)(2,1)}, u32[]{:S(2)}) copy-start(bf16[128,256]{1,0:T(8,128)(2,1)} %param.17) | copy-start | bytes 196612
  118.7 99.5 %copy-start.1 = (bf16[96,128,128]{2,1,0:T(8,128)(2,1)S(1)}, bf16[96,128,128]{2,1,0:T(8,128)(2,1)}, u32[]{:S(2)}) copy-start(bf16[96,128,128]{2,1,0:T(8,128)(2,1)} %get-tuple-element.327) | copy-start | bytes 9437188
  209.4 49.5 %all-to-all-start = ((bf16[16,128,256]{2,1,0:T(8,128)(2,1)}), bf16[16,128,256]{2,1,0:T(8,128)(2,1)}, u32[]{:S(2)}, u32[]{:S(2)}) async-start(bf16[16,128,256]{2,1,0:T(8,128)(2,1)} %tile.2), calls=%async_computation.1 | async-start | bytes 2097152 | tf_op jit(solution)/shard_map/all_to_all | solution.py:67
  218.1 2.9 copy-start.2
  218.1 470.3 %all-reduce.2.cloned.1.call-start = ((), (), s32[]{:S(2)}) async-start(), calls=%async_computation.5 | async-start | bytes 524288 | tf_op jit(solution)/shard_map/psum | solution.py:63
  221.9 568.8 %reduce-scatter.5.cloned.1.call-start = ((), (), s32[]{:S(2)}) async-start(), calls=%async_computation.6 | async-start | bytes 2162688 | tf_op jit(solution)/shard_map/reduce_scatter | solution.py:75
Sparse Core Ops, SparseCore 0:
  11.1 63.1 all-gather.1
  118.8 87.5 reduce-scatter.2
  225.8 462.5 all-reduce.1
  693.3 97.3 reduce-scatter.4
